TPU v7x, 32 devices: a whole 2x2x4 slice. The times are simulated.
32 devices in a mesh: gx: 4 (over y, core), yz: 8 (over z, x).
Axes of the slice: x: 2, y: 2, z: 4, core: 2. Of those that a mesh axis runs over, the one named last changes fastest.
Arguments:
- flow_speed_field: float32 [3, 32, 64, 128], P(None, 'gx', 'yz'), may hold values from -6 to 6
- thermal_field: float32 [32, 64, 128], P('gx', 'yz'), may hold values from 0.5 to 2
- walker_speed_vectors: float32 [3, 4096, 128], P(None, ('gx', 'yz')), may hold values from -6 to 6
- walker_statistical_mass: float32 [4096, 128], P(('gx', 'yz')), may hold values from 0.5 to 2
- gaussian_samples: float32 [2, 3, 4096, 128], P(None, None, ('gx', 'yz')), may hold values from -6 to 6
- walker_strip_position: int32 [4096, 128], P(('gx', 'yz')), may hold values from 0 to 127
- group_active_tally: int32 [4096], P(('gx', 'yz')), may hold values from 32 to 128
- group_resident_strip: int32 [4096], P(('gx', 'yz')), may hold values from 0 to 63
- migrating_group_table: int32 [512], P(('gx', 'yz')), may hold values from 0 to 127, as said below
- target_processor_slot: int32 [512, 1], P(('gx', 'yz')), may hold values from 0 to 7; in each aligned block of 16 rows (0 to 15, 16 to 31, ...) at most 4 rows name the same one
- entered_strip_slot: int32 [512], P(('gx', 'yz')), may hold values from 0 to 63
Outputs:
- new_fields: float32 [4, 32, 64, 128], P(None, 'gx', 'yz')
- particle_velocity: float32 [3, 4096, 128], P(None, ('gx', 'yz'))
Inputs may be any that keep to these rules, and one draw needn't show every extreme that they name: `migrating_group_table`: within each device's 16 entries the block indices are distinct. `target_processor_slot`: among the 16 rows of one device no yz index appears more than 4 times.
All inputs are finite; a program needn't handle non-finite values.
Results may differ from a plain program's by a relative error of at most 0.00005.
Values sent between devices are 32-bit elements; how exact they have to be, the bound alone decides.
A program may use at most 64 MiB of HBM per device.

v0:
```python
import math

import jax
import jax.numpy as jnp
from jax import lax
from jax.sharding import PartitionSpec as P

DECAY = 0.6
VISCOSITY = 0.05
COUPLING = 0.02
STRESS_GAIN = 0.005
RELAXATION = 0.5
HIGHEST = lax.Precision.HIGHEST
PAIRS = ((0, 0), (0, 1), (0, 2), (1, 1), (1, 2), (2, 2))
PAIR_INDEX = ((0, 1, 2), (1, 3, 4), (2, 4, 5))


def with_halo(block, sides, width):
    for axis, dim in sides:
        count = lax.axis_size(axis)
        forward = [(i, i + 1) for i in range(count - 1)]
        backward = [(target, source) for source, target in forward]
        low = lax.ppermute(
            lax.slice_in_dim(block, block.shape[dim] - width, None, axis=dim), axis, forward
        )
        high = lax.ppermute(lax.slice_in_dim(block, 0, width, axis=dim), axis, backward)
        block = jnp.concatenate([low, block, high], axis=dim)
    return block


def neighbour(padded, axis, offset):
    sizes = [padded.shape[1] - 2, padded.shape[2] - 2, padded.shape[3] - 2]
    begin = [1, 1, 1]
    begin[axis] = 1 + offset
    return padded[
        :,
        begin[0] : begin[0] + sizes[0],
        begin[1] : begin[1] + sizes[1],
        begin[2] : begin[2] + sizes[2],
    ]


def laplace(padded):
    total = neighbour(padded, 0, 1) + neighbour(padded, 0, -1)
    total = total + neighbour(padded, 1, 1) + neighbour(padded, 1, -1)
    total = total + neighbour(padded, 2, 1) + neighbour(padded, 2, -1)
    return total - 6.0 * neighbour(padded, 0, 0)


def fluid_step(padded_fields, padded_stress, moments):
    flow = neighbour(padded_fields, 0, 0)[:3]
    heat = neighbour(padded_fields, 0, 0)[3]
    density = moments[0]
    momentum = moments[1:4]
    stress = moments[4:10]
    smooth = laplace(padded_fields)
    slopes = [
        0.5 * (neighbour(padded_stress, axis, 1) - neighbour(padded_stress, axis, -1))
        for axis in range(3)
    ]
    divergence = jnp.stack(
        [
            slopes[0][PAIR_INDEX[row][0]]
            + slopes[1][PAIR_INDEX[row][1]]
            + slopes[2][PAIR_INDEX[row][2]]
            for row in range(3)
        ]
    )
    new_flow = (
        flow
        + VISCOSITY * smooth[:3]
        + COUPLING * (momentum - density[None] * flow)
        - STRESS_GAIN * divergence
    )
    energy = (
        stress[0]
        + stress[3]
        + stress[5]
        - 2.0 * jnp.sum(momentum * flow, axis=0)
        + density * jnp.sum(flow * flow, axis=0)
    ) / 3.0
    new_heat = heat + VISCOSITY * smooth[3] + COUPLING * (energy - density * heat)
    return jnp.concatenate([new_flow, new_heat[None]], 0)


def drift_step(start, sampled, noise):
    return (
        sampled[:3]
        + DECAY * (start - sampled[:3])
        + jnp.sqrt((1.0 - DECAY * DECAY) * sampled[3])[None] * noise
    )


def pencil_table(pencils, count):
    return (pencils[:, None] == jnp.arange(count, dtype=jnp.int32)[None, :]).astype(jnp.float32)


def pencil_fields(grid, pencils):
    return jnp.einsum("np,cpz->cnz", pencil_table(pencils, grid.shape[1]), grid, precision=HIGHEST)


def at_cells(columns, cells):
    channels = columns.shape[0]
    count, slots = cells.shape
    width = columns.shape[2]
    group = math.gcd(count, 128)
    grouped_columns = columns.reshape(channels, count // group, group, width).transpose(1, 0, 2, 3)
    grouped_cells = cells.reshape(count // group, group, slots)

    def at_one_group(pair):
        values, where = pair
        onehot = (where[:, :, None] == jnp.arange(width, dtype=jnp.int32)[None, None, :]).astype(
            jnp.float32
        )
        return jnp.einsum("gsz,cgz->cgs", onehot, values, precision=HIGHEST)

    picked = lax.map(at_one_group, (grouped_columns, grouped_cells))
    return picked.transpose(1, 0, 2, 3).reshape(channels, count, slots)


def deposit(velocity_now, weight, cells, width):
    count, slots = weight.shape
    terms = (
        [weight]
        + [weight * velocity_now[row] for row in range(3)]
        + [weight * velocity_now[one] * velocity_now[two] for one, two in PAIRS]
    )
    group = math.gcd(count, 128)
    stacked = jnp.stack(terms, axis=1).reshape(count // group, group, 10, slots)
    grouped_cells = cells.reshape(count // group, group, slots)

    def deposit_one_group(pair):
        values, where = pair
        onehot = (where[:, :, None] == jnp.arange(width, dtype=jnp.int32)[None, None, :]).astype(
            jnp.float32
        )
        return jnp.einsum("gks,gsz->gkz", values, onehot, precision=HIGHEST)

    return lax.map(deposit_one_group, (stacked, grouped_cells)).reshape(count, 10, width)


def advance(mesh_element_measure, moments):
    padded = with_halo(
        jnp.concatenate([mesh_element_measure, moments[4:10]], 0), (("gx", 1), ("yz", 2)), 1
    )
    padded = jnp.pad(padded, ((0, 0), (0, 0), (0, 0), (1, 1)))
    return fluid_step(padded[:4], padded[4:], moments)


def shards(
    flow_speed_field,
    thermal_field,
    walker_speed_vectors,
    walker_statistical_mass,
    gaussian_samples,
    walker_strip_position,
    group_active_tally,
    group_resident_strip,
    migrating_group_table,
    target_processor_slot,
    entered_strip_slot,
):
    yz_count = lax.axis_size("yz")
    spacing_along_x, spacing_along_y, spacing_along_z = thermal_field.shape
    block_count, slots = walker_statistical_mass.shape
    moving = migrating_group_table.shape[0]
    capacity = 2 * moving // yz_count
    received = yz_count * capacity
    pencil_count = spacing_along_x * spacing_along_y
    mesh_element_measure = jnp.concatenate([flow_speed_field, thermal_field[None]], 0)
    grid = mesh_element_measure.reshape(4, pencil_count, spacing_along_z)
    live = (
        lax.broadcasted_iota(jnp.int32, (block_count, slots), 1) < group_active_tally[:, None]
    ).astype(jnp.float32)
    weight = walker_statistical_mass * live
    home_columns = pencil_fields(grid, group_resident_strip)
    home = at_cells(home_columns, walker_strip_position)
    first_velocity = drift_step(walker_speed_vectors, home, gaussian_samples[0])
    target = target_processor_slot[:, 0]
    order_ids = jnp.arange(moving, dtype=jnp.int32)
    earlier = (target[:, None] == target[None, :]) & (order_ids[None, :] < order_ids[:, None])
    slot_of = target * capacity + jnp.sum(earlier.astype(jnp.int32), axis=1)
    staying = jnp.ones((block_count,), jnp.float32).at[migrating_group_table].set(0.0)
    slot_pencil = jnp.zeros((received,), jnp.int32).at[slot_of].set(entered_strip_slot)
    payload = jnp.concatenate(
        [
            first_velocity[:, migrating_group_table],
            weight[migrating_group_table][None],
            gaussian_samples[1][:, migrating_group_table],
        ],
        0,
    )
    outgoing = jnp.zeros((7, received, slots), jnp.float32).at[:, slot_of].set(payload)
    out_cells = (
        jnp.zeros((1, received, slots), jnp.int32)
        .at[0, slot_of]
        .set(walker_strip_position[migrating_group_table])
    )
    arrived, arrived_cells, arrived_pencils = (
        lax.all_to_all(
            outgoing.reshape(7, yz_count, capacity, slots),
            "yz",
            split_axis=1,
            concat_axis=1,
            tiled=True,
        ),
        lax.all_to_all(
            out_cells.reshape(1, yz_count, capacity, slots),
            "yz",
            split_axis=1,
            concat_axis=1,
            tiled=True,
        ),
        lax.all_to_all(
            slot_pencil.reshape(1, yz_count, capacity),
            "yz",
            split_axis=1,
            concat_axis=1,
            tiled=True,
        ),
    )
    arrived = arrived.reshape(7, received, slots)
    arrived_cells = arrived_cells.reshape(received, slots)
    arrived_pencils = arrived_pencils.reshape(received)
    all_pencils = jnp.concatenate([group_resident_strip, arrived_pencils])
    all_cells = jnp.concatenate([walker_strip_position, arrived_cells], 0)
    sampled = jnp.concatenate(
        [home, at_cells(pencil_fields(grid, arrived_pencils), arrived_cells)], 1
    )
    start_velocity = jnp.concatenate([first_velocity, arrived[0:3]], 1)
    noise = jnp.concatenate([gaussian_samples[1], arrived[4:7]], 1)
    second_velocity = drift_step(start_velocity, sampled, noise)
    all_weight = jnp.concatenate([weight * staying[:, None], arrived[3]], 0)
    per_block = deposit(second_velocity, all_weight, all_cells, spacing_along_z)
    moments = jnp.einsum(
        "np,nkz->kpz", pencil_table(all_pencils, pencil_count), per_block, precision=HIGHEST
    )
    new_cube = advance(
        mesh_element_measure, moments.reshape(10, spacing_along_x, spacing_along_y, spacing_along_z)
    )
    new_grid = new_cube.reshape(4, pencil_count, spacing_along_z)
    after = at_cells(pencil_fields(new_grid, all_pencils), all_cells)
    third_velocity = second_velocity + RELAXATION * (after[:3] - second_velocity)
    returned = lax.all_to_all(
        third_velocity[:, block_count:].reshape(3, yz_count, capacity, slots),
        "yz",
        split_axis=1,
        concat_axis=1,
        tiled=True,
    )
    returned = returned.reshape(3, received, slots)
    final = third_velocity[:, :block_count].at[:, migrating_group_table].set(returned[:, slot_of])
    return (new_cube, final * live[None])


def solution(mesh):
    return jax.shard_map(
        shards,
        mesh=mesh,
        in_specs=(
            P(None, "gx", "yz", None),
            P("gx", "yz", None),
            P(None, ("gx", "yz"), None),
            P(("gx", "yz"), None),
            P(None, None, ("gx", "yz"), None),
            P(("gx", "yz"), None),
            P(("gx", "yz")),
            P(("gx", "yz")),
            P(("gx", "yz")),
            P(("gx", "yz"), None),
            P(("gx", "yz")),
        ),
        out_specs=(P(None, "gx", "yz", None), P(None, ("gx", "yz"), None)),
        check_vma=False,
    )
```

profile of v0, /device:TPU:0, one launch (start us, length us, event | category | flops | bytes accessed | tf_op | source)
XLA Modules:
  0.0 101.9 jit_solution(5623307249634993809)
XLA Ops:
  3.6 7.3 %all-to-all-start.1 = ((s32[1,8,4]{2,0,1:T(1,128)}), s32[1,8,4]{2,0,1:T(1,128)S(1)}, u32[]{:S(2)}, u32[]{:S(2)}) async-start(s32[1,8,4]{2,0,1:T(1,128)} %bitcast.29), calls=%async_computation.1 | async-start | bytes 8192 | tf_op jit(solution)/shard_map/all_to_all | solution.py:214
  12.5 8.8 %fusion.15 = f32[4,128,128]{2,0,1:T(4,128)S(1)} fusion(f32[4,128,128]{2,0,1:T(4,128)S(1)} %copy.133, s32[128,128]{1,0:T(8,128)} %param.20), kind=kOutput, calls=%fused_computation.42 | convolution fusion | flops 102760448 | bytes 589824 | tf_op jit(solution)/shard_map/while/body/eval_jaxpr/gsz,cgz->cgs/dot_general | solution.py:115
  27.7 6.0 %all-to-all-start.2 = ((s32[1,8,4,128]{3,2,0,1:T(4,128)}), s32[1,8,4,128]{3,2,0,1:T(4,128)S(1)}, u32[]{:S(2)}, u32[]{:S(2)}) async-start(s32[1,8,4,128]{3,2,0,1:T(4,128)} %bitcast.32), calls=%async_computation.2 | async-start | bytes 32768 | tf_op jit(solution)/shard_map/all_to_all | solution.py:207
  35.2 5.0 %all-to-all-done.2 = s32[1,8,4,128]{3,2,0,1:T(4,128)S(1)} async-done(((s32[1,8,4,128]{3,2,0,1:T(4,128)}), s32[1,8,4,128]{3,2,0,1:T(4,128)S(1)}, u32[]{:S(2)}, u32[]{:S(2)}) %all-to-all-start.2) | async-done | bytes 16416 | tf_op jit(solution)/shard_map/all_to_all | solution.py:207
  40.2 3.4 %all-to-all-start = ((f32[7,8,4,128]{3,2,0,1:T(4,128)}), f32[7,8,4,128]{3,2,0,1:T(4,128)S(1)}, u32[]{:S(2)}, u32[]{:S(2)}) async-start(f32[7,8,4,128]{3,2,0,1:T(4,128)} %copy.137), calls=%async_computation | async-start | bytes 229376 | tf_op jit(solution)/shard_map/all_to_all | solution.py:200
  43.6 2.0 %fusion.16 = f32[4,32,128]{2,0,1:T(4,128)S(1)} fusion(s32[32,128]{1,0:T(8,128)S(1)} %bitcast.200, f32[4,32,128]{2,1,0:T(8,128)S(1)} %convolution_bitcast_fusion.2), kind=kOutput, calls=%fused_computation.44 | convolution fusion | flops 25690112 | bytes 147456 | tf_op jit(solution)/shard_map/while/body/eval_jaxpr/gsz,cgz->cgs/dot_general | solution.py:115
  45.9 4.9 %all-to-all-done = f32[7,8,4,128]{3,2,0,1:T(4,128)S(1)} async-done(((f32[7,8,4,128]{3,2,0,1:T(4,128)}), f32[7,8,4,128]{3,2,0,1:T(4,128)S(1)}, u32[]{:S(2)}, u32[]{:S(2)}) %all-to-all-start) | async-done | bytes 114720 | tf_op jit(solution)/shard_map/all_to_all | solution.py:200
  51.5 9.5 %while.4 = (s32[]{:T(128)}, f32[5,32,10,128]{3,2,1,0:T(8,128)S(1)}, f32[5,32,10,128]{3,1,2,0:T(8,128)S(1)}, s32[5,32,128]{2,1,0:T(8,128)S(1)}, s32[]{:T(128)}) while((s32[]{:T(128)}, f32[5,32,10,128]{3,2,1,0:T(8,128)S(1)}, f32[5,32,10,128]{3,1,2,0:T(8,128)S(1)}, s32[5,32,128]{2,1,0:T(8,128)S(1)}, s32[]{:T(128)}) %tuple.64), condition=%wide.region_6.7_spmd, body=%wide.region_5.6_spmd.sunk | while | flops 63438848 | bytes 802889 | solution.py:139
  51.6 1.8 %fusion.87 = f32[5,32,10,128]{3,2,1,0:T(8,128)S(1)} fusion(f32[5,32,10,128]{3,2,1,0:T(8,128)S(1)} %get-tuple-element.181, s32[]{:T(128)} %get-tuple-element.180, s32[32,128]{1,0:T(8,128)S(1)} %dynamic-slice_bitcast_fusion.4, f32[1,32,10,128]{3,1,2,0:T(8,128)S(1)} %constant_dynamic-slice_fusion.2), kind=kOutput, calls=%fused_computation.13.clone.1 | convolution fusion | flops 63438848 | bytes 442372 | tf_op jit(solution)/shard_map/while/body/eval_jaxpr/gks,gsz->gkz/dot_general | solution.py:137
  53.5 1.8 %fusion.87 = f32[5,32,10,128]{3,2,1,0:T(8,128)S(1)} fusion(f32[5,32,10,128]{3,2,1,0:T(8,128)S(1)} %get-tuple-element.181, s32[]{:T(128)} %get-tuple-element.180, s32[32,128]{1,0:T(8,128)S(1)} %dynamic-slice_bitcast_fusion.4, f32[1,32,10,128]{3,1,2,0:T(8,128)S(1)} %constant_dynamic-slice_fusion.2), kind=kOutput, calls=%fused_computation.13.clone.1 | convolution fusion | flops 63438848 | bytes 442372 | tf_op jit(solution)/shard_map/while/body/eval_jaxpr/gks,gsz->gkz/dot_general | solution.py:137
  55.4 1.8 %fusion.87 = f32[5,32,10,128]{3,2,1,0:T(8,128)S(1)} fusion(f32[5,32,10,128]{3,2,1,0:T(8,128)S(1)} %get-tuple-element.181, s32[]{:T(128)} %get-tuple-element.180, s32[32,128]{1,0:T(8,128)S(1)} %dynamic-slice_bitcast_fusion.4, f32[1,32,10,128]{3,1,2,0:T(8,128)S(1)} %constant_dynamic-slice_fusion.2), kind=kOutput, calls=%fused_computation.13.clone.1 | convolution fusion | flops 63438848 | bytes 442372 | tf_op jit(solution)/shard_map/while/body/eval_jaxpr/gks,gsz->gkz/dot_general | solution.py:137
  57.3 1.8 %fusion.87 = f32[5,32,10,128]{3,2,1,0:T(8,128)S(1)} fusion(f32[5,32,10,128]{3,2,1,0:T(8,128)S(1)} %get-tuple-element.181, s32[]{:T(128)} %get-tuple-element.180, s32[32,128]{1,0:T(8,128)S(1)} %dynamic-slice_bitcast_fusion.4, f32[1,32,10,128]{3,1,2,0:T(8,128)S(1)} %constant_dynamic-slice_fusion.2), kind=kOutput, calls=%fused_computation.13.clone.1 | convolution fusion | flops 63438848 | bytes 442372 | tf_op jit(solution)/shard_map/while/body/eval_jaxpr/gks,gsz->gkz/dot_general | solution.py:137
  59.2 1.8 %fusion.87 = f32[5,32,10,128]{3,2,1,0:T(8,128)S(1)} fusion(f32[5,32,10,128]{3,2,1,0:T(8,128)S(1)} %get-tuple-element.181, s32[]{:T(128)} %get-tuple-element.180, s32[32,128]{1,0:T(8,128)S(1)} %dynamic-slice_bitcast_fusion.4, f32[1,32,10,128]{3,1,2,0:T(8,128)S(1)} %constant_dynamic-slice_fusion.2), kind=kOutput, calls=%fused_computation.13.clone.1 | convolution fusion | flops 63438848 | bytes 442372 | tf_op jit(solution)/shard_map/while/body/eval_jaxpr/gks,gsz->gkz/dot_general | solution.py:137
  63.1 3.0 %collective-permute-start.1 = (f32[10,1,8,128]{3,2,1,0:T(8,128)S(1)}, f32[10,1,8,128]{3,2,1,0:T(8,128)S(1)}, u32[]{:S(2)}, u32[]{:S(2)}) collective-permute-start(f32[10,1,8,128]{3,2,1,0:T(8,128)S(1)} %get-tuple-element.116), channel_id=1, source_target_pairs={{0,8},{8,16},{16,24},{1,9},{9,17},{17,25},{2,10},{10,18},{18,26},{... | collective-permute-start | bytes 122888 | tf_op jit(solution)/shard_map/ppermute | solution.py:23
  68.3 4.5 %collective-permute-start.3 = (f32[10,10,1,128]{3,2,1,0:T(1,128)S(1)}, f32[10,10,1,128]{3,2,1,0:T(1,128)S(1)}, u32[]{:S(2)}, u32[]{:S(2)}) collective-permute-start(f32[10,10,1,128]{3,2,1,0:T(1,128)S(1)} %get-tuple-element.112), channel_id=1, source_target_pairs={{0,1},{1,2},{2,3},{3,4},{4,5},{5,6},{6,7},{8,9},{9,10},{10,11},{11... | collective-permute-start | bytes 153608 | tf_op jit(solution)/shard_map/ppermute | solution.py:23
  73.2 1.7 %collective-permute-done.3 = f32[10,10,1,128]{3,2,1,0:T(1,128)S(1)} collective-permute-done((f32[10,10,1,128]{3,2,1,0:T(1,128)S(1)}, f32[10,10,1,128]{3,2,1,0:T(1,128)S(1)}, u32[]{:S(2)}, u32[]{:S(2)}) %collective-permute-start.3) | collective-permute-done | bytes 51232 | tf_op jit(solution)/shard_map/ppermute | solution.py:23
  76.8 10.2 %while.5 = (s32[]{:T(128)}, f32[5,4,32,128]{3,1,2,0:T(4,128)S(1)}, f32[5,4,32,128]{3,1,2,0:T(4,128)S(1)}, s32[5,32,128]{2,1,0:T(8,128)S(1)}, s32[]{:T(128)}) while((s32[]{:T(128)}, f32[5,4,32,128]{3,1,2,0:T(4,128)S(1)}, f32[5,4,32,128]{3,1,2,0:T(4,128)S(1)}, s32[5,32,128]{2,1,0:T(8,128)S(1)}, s32[]{:T(128)}) %tuple.66), condition=%wide.region_10.11_spmd, body=%wide.region_9.10_spmd.sunk | while | flops 25690112 | bytes 181313 | solution.py:117
  76.8 2.0 %fusion.89 = f32[5,4,32,128]{3,1,2,0:T(4,128)S(1)} fusion(f32[5,4,32,128]{3,1,2,0:T(4,128)S(1)} %get-tuple-element.196, s32[]{:T(128)} %get-tuple-element.195, s32[32,128]{1,0:T(8,128)S(1)} %dynamic-slice_bitcast_fusion.5, f32[5,4,32,128]{3,1,2,0:T(4,128)S(1)} %get-tuple-element.202), kind=kOutput, calls=%fused_computation.21.clone.1 | convolution fusion | flops 25690112 | bytes 148480 | tf_op jit(solution)/shard_map/while/body/eval_jaxpr/gsz,cgz->cgs/dot_general | solution.py:115
  78.9 2.0 %fusion.89 = f32[5,4,32,128]{3,1,2,0:T(4,128)S(1)} fusion(f32[5,4,32,128]{3,1,2,0:T(4,128)S(1)} %get-tuple-element.196, s32[]{:T(128)} %get-tuple-element.195, s32[32,128]{1,0:T(8,128)S(1)} %dynamic-slice_bitcast_fusion.5, f32[5,4,32,128]{3,1,2,0:T(4,128)S(1)} %get-tuple-element.202), kind=kOutput, calls=%fused_computation.21.clone.1 | convolution fusion | flops 25690112 | bytes 148480 | tf_op jit(solution)/shard_map/while/body/eval_jaxpr/gsz,cgz->cgs/dot_general | solution.py:115
  80.9 2.0 %fusion.89 = f32[5,4,32,128]{3,1,2,0:T(4,128)S(1)} fusion(f32[5,4,32,128]{3,1,2,0:T(4,128)S(1)} %get-tuple-element.196, s32[]{:T(128)} %get-tuple-element.195, s32[32,128]{1,0:T(8,128)S(1)} %dynamic-slice_bitcast_fusion.5, f32[5,4,32,128]{3,1,2,0:T(4,128)S(1)} %get-tuple-element.202), kind=kOutput, calls=%fused_computation.21.clone.1 | convolution fusion | flops 25690112 | bytes 148480 | tf_op jit(solution)/shard_map/while/body/eval_jaxpr/gsz,cgz->cgs/dot_general | solution.py:115
  82.9 2.0 %fusion.89 = f32[5,4,32,128]{3,1,2,0:T(4,128)S(1)} fusion(f32[5,4,32,128]{3,1,2,0:T(4,128)S(1)} %get-tuple-element.196, s32[]{:T(128)} %get-tuple-element.195, s32[32,128]{1,0:T(8,128)S(1)} %dynamic-slice_bitcast_fusion.5, f32[5,4,32,128]{3,1,2,0:T(4,128)S(1)} %get-tuple-element.202), kind=kOutput, calls=%fused_computation.21.clone.1 | convolution fusion | flops 25690112 | bytes 148480 | tf_op jit(solution)/shard_map/while/body/eval_jaxpr/gsz,cgz->cgs/dot_general | solution.py:115
  85.0 2.0 %fusion.89 = f32[5,4,32,128]{3,1,2,0:T(4,128)S(1)} fusion(f32[5,4,32,128]{3,1,2,0:T(4,128)S(1)} %get-tuple-element.196, s32[]{:T(128)} %get-tuple-element.195, s32[32,128]{1,0:T(8,128)S(1)} %dynamic-slice_bitcast_fusion.5, f32[5,4,32,128]{3,1,2,0:T(4,128)S(1)} %get-tuple-element.202), kind=kOutput, calls=%fused_computation.21.clone.1 | convolution fusion | flops 25690112 | bytes 148480 | tf_op jit(solution)/shard_map/while/body/eval_jaxpr/gsz,cgz->cgs/dot_general | solution.py:115
  87.9 4.8 %all-to-all-start.3 = ((f32[3,8,4,128]{3,2,0,1:T(4,128)}), f32[3,8,4,128]{3,2,0,1:T(4,128)S(1)}, u32[]{:S(2)}, u32[]{:S(2)}) async-start(f32[3,8,4,128]{3,2,0,1:T(4,128)} %copy.145), calls=%async_computation.3 | async-start | bytes 98304 | tf_op jit(solution)/shard_map/all_to_all | solution.py:244
  93.3 6.1 %all-to-all-done.3 = f32[3,8,4,128]{3,2,0,1:T(4,128)S(1)} async-done(((f32[3,8,4,128]{3,2,0,1:T(4,128)}), f32[3,8,4,128]{3,2,0,1:T(4,128)S(1)}, u32[]{:S(2)}, u32[]{:S(2)}) %all-to-all-start.3) | async-done | bytes 49184 | tf_op jit(solution)/shard_map/all_to_all | solution.py:244
  (116 shorter events, 23.5 us)
Async XLA Ops:
  3.6 24.0 %all-to-all-start.1 = ((s32[1,8,4]{2,0,1:T(1,128)}), s32[1,8,4]{2,0,1:T(1,128)S(1)}, u32[]{:S(2)}, u32[]{:S(2)}) async-start(s32[1,8,4]{2,0,1:T(1,128)} %bitcast.29), calls=%async_computation.1 | async-start | bytes 8192 | tf_op jit(solution)/shard_map/all_to_all | solution.py:214
  10.9 10.5 %copy-start.2 = (f32[2,3,128,128]{3,2,1,0:T(8,128)S(1)}, f32[2,3,128,128]{3,2,1,0:T(8,128)}, u32[]{:S(2)}) copy-start(f32[2,3,128,128]{3,2,1,0:T(8,128)} %param.19) | copy-start | bytes 1179652
  12.4 9.1 %copy-start.8 = (s32[16]{0:T(128)S(1)}, s32[16]{0:T(128)}, u32[]{:S(2)}) copy-start(s32[16]{0:T(128)} %param.23) | copy-start | bytes 196
  12.5 9.1 %copy-start.5 = (s32[128,128]{1,0:T(8,128)S(1)}, s32[128,128]{1,0:T(8,128)}, u32[]{:S(2)}) copy-start(s32[128,128]{1,0:T(8,128)} %param.20) | copy-start | bytes 196612
  12.5 10.4 %copy-start.3 = (f32[3,128,128]{2,1,0:T(8,128)S(1)}, f32[3,128,128]{2,1,0:T(8,128)}, u32[]{:S(2)}) copy-start(f32[3,128,128]{2,1,0:T(8,128)} %param.17) | copy-start | bytes 589828
  12.5 11.3 %copy-start.6 = (s32[128]{0:T(128)S(1)}, s32[128]{0:T(128)}, u32[]{:S(2)}) copy-start(s32[128]{0:T(128)} %param.21) | copy-start | bytes 1540
  12.5 12.0 %copy-start.4 = (f32[128,128]{1,0:T(8,128)S(1)}, f32[128,128]{1,0:T(8,128)}, u32[]{:S(2)}) copy-start(f32[128,128]{1,0:T(8,128)} %param.18) | copy-start | bytes 196612
  21.5 13.4 %copy-start = (f32[3,8,8,128]{3,2,1,0:T(8,128)S(1)}, f32[3,8,8,128]{3,2,1,0:T(8,128)}, u32[]{:S(2)}) copy-start(f32[3,8,8,128]{3,2,1,0:T(8,128)} %param.15) | copy-start | bytes 294916
  21.5 13.4 %copy-start.1 = (f32[8,8,128]{2,1,0:T(8,128)S(1)}, f32[8,8,128]{2,1,0:T(8,128)}, u32[]{:S(2)}) copy-start(f32[8,8,128]{2,1,0:T(8,128)} %param.16) | copy-start | bytes 98308
  21.5 13.6 %copy-start.7 = (s32[128]{0:T(128)S(1)}, s32[128]{0:T(128)}, u32[]{:S(2)}) copy-start(s32[128]{0:T(128)} %param.22) | copy-start | bytes 1540
  27.7 12.6 %all-to-all-start.2 = ((s32[1,8,4,128]{3,2,0,1:T(4,128)}), s32[1,8,4,128]{3,2,0,1:T(4,128)S(1)}, u32[]{:S(2)}, u32[]{:S(2)}) async-start(s32[1,8,4,128]{3,2,0,1:T(4,128)} %bitcast.32), calls=%async_computation.2 | async-start | bytes 32768 | tf_op jit(solution)/shard_map/all_to_all | solution.py:207
  40.2 10.5 %all-to-all-start = ((f32[7,8,4,128]{3,2,0,1:T(4,128)}), f32[7,8,4,128]{3,2,0,1:T(4,128)S(1)}, u32[]{:S(2)}, u32[]{:S(2)}) async-start(f32[7,8,4,128]{3,2,0,1:T(4,128)} %copy.137), calls=%async_computation | async-start | bytes 229376 | tf_op jit(solution)/shard_map/all_to_all | solution.py:200
  61.8 4.4 %collective-permute-start = (f32[10,1,8,128]{3,2,1,0:T(8,128)S(1)}, f32[10,1,8,128]{3,2,1,0:T(8,128)S(1)}, u32[]{:S(2)}, u32[]{:S(2)}) collective-permute-start(f32[10,1,8,128]{3,2,1,0:T(8,128)S(1)} %get-tuple-element.117), channel_id=1, source_target_pairs={{8,0},{16,8},{24,16},{9,1},{17,9},{25,17},{10,2},{18,10},{26,18},{... | collective-permute-start | bytes 122888 | tf_op jit(solution)/shard_map/ppermute | solution.py:26
  63.1 3.9 %collective-permute-start.1 = (f32[10,1,8,128]{3,2,1,0:T(8,128)S(1)}, f32[10,1,8,128]{3,2,1,0:T(8,128)S(1)}, u32[]{:S(2)}, u32[]{:S(2)}) collective-permute-start(f32[10,1,8,128]{3,2,1,0:T(8,128)S(1)} %get-tuple-element.116), channel_id=1, source_target_pairs={{0,8},{8,16},{16,24},{1,9},{9,17},{17,25},{2,10},{10,18},{18,26},{... | collective-permute-start | bytes 122888 | tf_op jit(solution)/shard_map/ppermute | solution.py:23
  67.0 6.2 %collective-permute-start.2 = (f32[10,10,1,128]{3,2,1,0:T(1,128)S(1)}, f32[10,10,1,128]{3,2,1,0:T(1,128)S(1)}, u32[]{:S(2)}, u32[]{:S(2)}) collective-permute-start(f32[10,10,1,128]{3,2,1,0:T(1,128)S(1)} %get-tuple-element.113), channel_id=1, source_target_pairs={{1,0},{2,1},{3,2},{4,3},{5,4},{6,5},{7,6},{9,8},{10,9},{11,10},{12... | collective-permute-start | bytes 153608 | tf_op jit(solution)/shard_map/ppermute | solution.py:26
  68.3 6.6 %collective-permute-start.3 = (f32[10,10,1,128]{3,2,1,0:T(1,128)S(1)}, f32[10,10,1,128]{3,2,1,0:T(1,128)S(1)}, u32[]{:S(2)}, u32[]{:S(2)}) collective-permute-start(f32[10,10,1,128]{3,2,1,0:T(1,128)S(1)} %get-tuple-element.112), channel_id=1, source_target_pairs={{0,1},{1,2},{2,3},{3,4},{4,5},{5,6},{6,7},{8,9},{9,10},{10,11},{11... | collective-permute-start | bytes 153608 | tf_op jit(solution)/shard_map/ppermute | solution.py:23
  87.9 11.6 %all-to-all-start.3 = ((f32[3,8,4,128]{3,2,0,1:T(4,128)}), f32[3,8,4,128]{3,2,0,1:T(4,128)S(1)}, u32[]{:S(2)}, u32[]{:S(2)}) async-start(f32[3,8,4,128]{3,2,0,1:T(4,128)} %copy.145), calls=%async_computation.3 | async-start | bytes 98304 | tf_op jit(solution)/shard_map/all_to_all | solution.py:244
where the time goes:
time: 103 us; the launch traced here: 102 us
  matrix products  32.7 us (32%)
  starting transfers between devices  31.6 us (31%)
  waiting for transfers between devices  18.9 us (18%)
  local copies, waits for them, and re-layouts  11.4 us (11%)
  other arithmetic  5.86 us (6%)
  between operations  1.25 us (1%)
    dot_general x7, matrix products, at_one_group(): return jnp.einsum('gsz,cgz->cgs', onehot, values, precision=HIGHEST)  20.9 us
    dot_general x5, matrix products, deposit_one_group(): return jnp.einsum('gks,gsz->gkz', values, onehot, precision=HIGHEST)  9.22 us
    ppermute x2, starting transfers between devices, with_halo(): lax.ppermute(lax.slice_in_dim(block, block.shape[dim] - width, None, axis...  7.58 us
    all_to_all x1, starting transfers between devices, shards(): lax.all_to_all(slot_pencil.reshape(1, yz_count, capacity), 'yz', split_ax...  7.28 us
    all_to_all x1, waiting for transfers between devices, shards(): lax.all_to_all(third_velocity[:, block_count:].reshape(3, yz_count, capac...  6.13 us
    all_to_all x1, starting transfers between devices, shards(): lax.all_to_all(out_cells.reshape(1, yz_count, capacity, slots), 'yz', spl...  5.99 us
    all_to_all x1, waiting for transfers between devices, shards(): lax.all_to_all(out_cells.reshape(1, yz_count, capacity, slots), 'yz', spl...  5.05 us
    all_to_all x1, waiting for transfers between devices, shards(): lax.all_to_all(outgoing.reshape(7, yz_count, capacity, slots), 'yz', spli...  4.9 us
  transfers between devices with their start and end apart: 8, of which 6 were waited for; matrix products, arithmetic and copies ran while one was open for 20% of the time, Pallas kernels for 0%

commit v1 on v0

v1 whole, which is shorter than its diff:
```python
import functools

import jax
import jax.numpy as jnp
from jax import lax
from jax.experimental import pallas as pl
from jax.experimental.pallas import tpu as pltpu
from jax.sharding import PartitionSpec as P

DECAY = 0.6
VISCOSITY = 0.05
COUPLING = 0.02
STRESS_GAIN = 0.005
RELAXATION = 0.5
PAIRS = ((0, 0), (0, 1), (0, 2), (1, 1), (1, 2), (2, 2))
PAIR_INDEX = ((0, 1, 2), (1, 3, 4), (2, 4, 5))
MOMENTS = 10
PITCH = 16
SENT = 9
MESH = pl.DeviceIdType.MESH
BF16 = jnp.bfloat16
F32 = jnp.float32


def split3(x):
    high = x.astype(BF16)
    rest = x - high.astype(F32)
    mid = rest.astype(BF16)
    low = (rest - mid.astype(F32)).astype(BF16)
    return high, mid, low


def dot(a, b):
    return jnp.dot(a, b, preferred_element_type=F32)


def dot_last(a, b):
    return lax.dot_general(a, b, (((1,), (1,)), ((), ())), preferred_element_type=F32)


def pick(onehot, x):
    high, mid, low = split3(x)
    return dot(onehot, high) + dot(onehot, mid) + dot(onehot, low)


def lanes(x, index):
    return jnp.take_along_axis(x, index, axis=1, mode="promise_in_bounds")


def onehot(condition):
    return jnp.where(condition, 1.0, 0.0)


def drift(start, u, spread, noise):
    return u + DECAY * (start - u) + spread * noise


def deposit(count, unroll, v_ref, cells_ref, pb_ref):
    width = v_ref.shape[1]
    slots = cells_ref.shape[1]
    where = lax.broadcasted_iota(jnp.int32, (width, slots), 0)

    def some(step, carry):
        for t in range(unroll):
            n = step * unroll + t
            row = pl.ds(pl.multiple_of(n * PITCH, PITCH), PITCH)
            lhs = jnp.concatenate(split3(v_ref[row, :]), axis=0)
            hot = onehot(cells_ref[pl.ds(n, 1), :] == where).astype(BF16)
            out = dot_last(lhs, hot)
            pb_ref[row, :] = out[:PITCH] + out[PITCH : 2 * PITCH] + out[2 * PITCH :]
        return carry

    lax.fori_loop(0, count // unroll, some, 0)


def put_terms(v_ref, count, weight, second):
    terms = (
        [weight]
        + [weight * second[row] for row in range(3)]
        + [weight * second[one] * second[two] for one, two in PAIRS]
    )
    for k, term in enumerate(terms):
        v_ref[pl.ds(k, count, stride=PITCH), :] = term


def kernel(
    n,
    n_gx,
    spans,
    flow,
    heat,
    speed,
    mass,
    noise,
    cells,
    tally,
    home,
    table,
    target,
    entered,
    fields_out,
    speed_out,
    v_ref,
    pb_ref,
    second_ref,
    cells_a,
    moments,
    wide,
    face_send,
    face_recv,
    stress_send,
    stress_recv,
    out_ref,
    in_ref,
    back_send,
    back_recv,
    out_s,
    out_r,
    face_s,
    face_r,
    stress_s,
    stress_r,
    back_s,
    back_r,
):
    X, Y, Z = spans
    pencils = X * Y
    blocks, slots = mass.shape
    moving = table.shape[1]
    cap = 2 * moving // n
    received = n * cap
    rows = out_ref.shape[0] // n
    back_rows = back_send.shape[0] // n
    gx = lax.axis_index("gx")
    me = lax.axis_index("yz")
    peers = [(i, lax.rem(me + i, n), lax.rem(me + n - i, n)) for i in range(1, n)]

    barrier = pltpu.get_barrier_semaphore()
    for _, peer, _ in peers:
        pl.semaphore_signal(barrier, inc=1, device_id={"yz": peer}, device_id_type=MESH)

    @pl.when(gx > 0)
    def _():
        pl.semaphore_signal(barrier, inc=1, device_id={"gx": gx - 1}, device_id_type=MESH)

    @pl.when(gx < n_gx - 1)
    def _():
        pl.semaphore_signal(barrier, inc=1, device_id={"gx": gx + 1}, device_id_type=MESH)

    sides = (
        (0, 1, gx > 0, gx == 0, {"gx": gx - 1}),
        (1, 0, gx < n_gx - 1, gx == n_gx - 1, {"gx": gx + 1}),
        (2, 3, me > 0, me == 0, {"yz": me - 1}),
        (3, 2, me < n - 1, me == n - 1, {"yz": me + 1}),
    )
    for side, _, _, edge, _ in sides:

        @pl.when(edge)
        def _(side=side):
            face_recv[side] = jnp.zeros(face_recv.shape[1:], F32)
            stress_recv[side] = jnp.zeros(stress_recv.shape[1:], F32)

    def face_copy(side, other, where, send, recv, send_sem, recv_sem):
        return pltpu.make_async_remote_copy(
            src_ref=send.at[side],
            dst_ref=recv.at[other],
            send_sem=send_sem.at[side],
            recv_sem=recv_sem.at[other],
            device_id=where,
            device_id_type=MESH,
        )

    def faces_start(send, recv, send_sem, recv_sem):
        for side, other, there, _, where in sides:

            @pl.when(there)
            def _(side=side, other=other, where=where):
                face_copy(side, other, where, send, recv, send_sem, recv_sem).start()

    def faces_wait(send, recv, send_sem, recv_sem):
        for side, _, there, _, where in sides:

            @pl.when(there)
            def _(side=side, where=where):
                face_copy(side, side, where, send, recv, send_sem, recv_sem).wait_recv()

    def faces_sent(send, recv, send_sem, recv_sem):
        for side, other, there, _, where in sides:

            @pl.when(there)
            def _(side=side, other=other, where=where):
                face_copy(side, other, where, send, recv, send_sem, recv_sem).wait_send()

    face_args = (face_send, face_recv, face_s, face_r)
    stress_args = (stress_send, stress_recv, stress_s, stress_r)

    def all_copy(i, peer, send, recv, height, send_sem, recv_sem):
        return pltpu.make_async_remote_copy(
            src_ref=send.at[pl.ds(pl.multiple_of(peer * height, 8), height), :],
            dst_ref=recv.at[pl.ds(pl.multiple_of(me * height, 8), height), :],
            send_sem=send_sem.at[i],
            recv_sem=recv_sem.at[i],
            device_id={"yz": peer},
            device_id_type=MESH,
        )

    def all_start(send, recv, height, send_sem, recv_sem):
        for i, peer, _ in peers:
            all_copy(i, peer, send, recv, height, send_sem, recv_sem).start()

    def all_wait(send, recv, height, send_sem, recv_sem):
        for i, _, source in peers:
            pltpu.make_async_remote_copy(
                src_ref=send.at[pl.ds(pl.multiple_of(source * height, 8), height), :],
                dst_ref=recv.at[pl.ds(pl.multiple_of(source * height, 8), height), :],
                send_sem=send_sem.at[i],
                recv_sem=recv_sem.at[i],
                device_id={"yz": source},
                device_id_type=MESH,
            ).wait_recv()

    def all_sent(send, recv, height, send_sem, recv_sem):
        for i, peer, _ in peers:
            all_copy(i, peer, send, recv, height, send_sem, recv_sem).wait_send()

    pay_args = (out_ref, in_ref, rows, out_s, out_r)
    back_args = (back_send, back_recv, back_rows, back_s, back_r)

    for c in range(4):
        grid = flow.at[c] if c < 3 else heat
        face_send[0, c] = grid[pl.ds(0, Y), :]
        face_send[1, c] = grid[pl.ds((X - 1) * Y, Y), :]
        face_send[2, c] = grid[pl.ds(0, X, stride=Y), :]
        face_send[3, c] = grid[pl.ds(Y - 1, X, stride=Y), :]

    iota = functools.partial(lax.broadcasted_iota, jnp.int32)
    eye = iota((moving, moving), 0) == iota((moving, moving), 1)
    target_row = target[...]
    target_col = jnp.sum(jnp.where(eye, target_row, 0), axis=1, keepdims=True)
    earlier = (target_col == target_row) & (iota((moving, moving), 0) < iota((moving, moving), 1))
    rank = jnp.sum(jnp.where(earlier, 1, 0), axis=0, keepdims=True)
    slot_row = rank * n + target_row
    slot_hot = onehot(iota((received, moving), 0) == slot_row)
    block_hot = onehot(iota((blocks, moving), 0) == table[...])
    from_block = dot_last(slot_hot.astype(BF16), block_hot.astype(BF16)).astype(BF16)
    to_block = dot_last(block_hot.astype(BF16), slot_hot.astype(BF16))
    moved = jnp.sum(to_block, axis=1, keepdims=True) > 0.5
    to_block = to_block.astype(BF16)
    pencil_out = jnp.sum(slot_hot * entered[...].astype(F32), axis=1, keepdims=True)

    home_t = onehot(iota((pencils, blocks), 0) == home[...])
    home_hot = home_t.T.astype(BF16)
    home_t = home_t.astype(BF16)
    live = onehot(iota((slots, blocks), 0) < tally[...]).T

    where = cells[...]
    u = [lanes(pick(home_hot, flow[c]), where) for c in range(3)]
    temp = lanes(pick(home_hot, heat[...]), where)
    spread = jnp.sqrt((1.0 - DECAY * DECAY) * temp)
    weight = mass[...] * live
    first = [drift(speed[c], u[c], spread, noise[c]) for c in range(3)]
    sent = [pick(from_block, first[c]) for c in range(3)]
    sent.append(pick(from_block, weight))
    sent += [pick(from_block, noise[3 + c]) for c in range(3)]
    sent.append(dot(from_block, where.astype(F32).astype(BF16)))
    sent.append(jnp.broadcast_to(pencil_out, (received, slots)))
    for c in range(SENT):
        for j in range(cap):
            out_ref[pl.ds(c * cap + j, n, stride=rows), :] = sent[c][j * n : (j + 1) * n]

    expected = n - 1 + jnp.where(gx > 0, 1, 0) + jnp.where(gx < n_gx - 1, 1, 0)
    pl.semaphore_wait(barrier, expected)
    all_start(*pay_args)
    faces_start(*face_args)
    own = pl.ds(pl.multiple_of(me * rows, 8), rows)
    in_ref[own, :] = out_ref[own, :]

    second = [drift(first[c], u[c], spread, noise[3 + c]) for c in range(3)]
    for c in range(3):
        second_ref[c] = second[c]
    put_terms(v_ref, blocks, jnp.where(moved, 0.0, weight), second)
    deposit(blocks, 8, v_ref, cells, pb_ref)
    for k in range(MOMENTS):
        moments[k] = pick(home_t, pb_ref[pl.ds(k, blocks, stride=PITCH), :])

    all_wait(*pay_args)
    got = [
        jnp.concatenate(
            [in_ref[pl.ds(c * cap + j, n, stride=rows), :] for j in range(cap)], axis=0
        )
        for c in range(SENT)
    ]
    where_a = got[7].astype(jnp.int32)
    cells_a[...] = where_a
    pencil_hot = onehot(got[8][:, :pencils].astype(jnp.int32) == iota((received, pencils), 1))
    pencil_t = pencil_hot.T.astype(BF16)
    pencil_hot = pencil_hot.astype(BF16)
    u_a = [lanes(pick(pencil_hot, flow[c]), where_a) for c in range(3)]
    temp_a = lanes(pick(pencil_hot, heat[...]), where_a)
    spread_a = jnp.sqrt((1.0 - DECAY * DECAY) * temp_a)
    second_a = [drift(got[c], u_a[c], spread_a, got[4 + c]) for c in range(3)]
    put_terms(v_ref, received, got[3], second_a)
    deposit(received, 8, v_ref, cells_a, pb_ref)
    for k in range(MOMENTS - 1, -1, -1):
        total = moments[k] + pick(pencil_t, pb_ref[pl.ds(k, received, stride=PITCH), :])
        moments[k] = total
        if k >= 4:
            s = k - 4
            stress_send[0, s] = total[:Y]
            stress_send[1, s] = total[pencils - Y :]
            stress_send[2, s] = moments[k, pl.ds(0, X, stride=Y), :]
            stress_send[3, s] = moments[k, pl.ds(Y - 1, X, stride=Y), :]
    faces_start(*stress_args)

    lane = iota((pencils, Z), 1)

    def along_z(x, step):
        if step > 0:
            return jnp.where(lane == Z - 1, 0.0, pltpu.roll(x, Z - 1, 1))
        return jnp.where(lane == 0, 0.0, pltpu.roll(x, 1, 1))

    def fill(slot, value, halo, c):
        wide[slot, 1 : X + 1, 8 : 8 + Y, :] = value.reshape(X, Y, Z)
        wide[slot, 0, 8 : 8 + Y, :] = halo[0, c]
        wide[slot, X + 1, 8 : 8 + Y, :] = halo[1, c]
        for x in range(X):
            wide[slot, x + 1, 7:8, :] = halo[2, c, x : x + 1]
            wide[slot, x + 1, 8 + Y : 9 + Y, :] = halo[3, c, x : x + 1]

    def along_x(slot, step):
        return wide[slot, 1 + step : 1 + step + X, 8 : 8 + Y, :].reshape(pencils, Z)

    def along_y(slot, step):
        return wide[slot, 1 : X + 1, 8 + step : 8 + step + Y, :].reshape(pencils, Z)

    faces_wait(*face_args)
    f = [flow[0], flow[1], flow[2], heat[...]]
    base = []
    for c in range(4):
        fill(c, f[c], face_recv, c)
        smooth = along_x(c, 1) + along_x(c, -1) + along_y(c, 1) + along_y(c, -1)
        smooth = smooth + along_z(f[c], 1) + along_z(f[c], -1) - 6.0 * f[c]
        base.append(f[c] + VISCOSITY * smooth)
    density = moments[0]
    momentum = [moments[1 + c] for c in range(3)]
    for c in range(3):
        base[c] = base[c] + COUPLING * (momentum[c] - density * f[c])
    dots = momentum[0] * f[0] + momentum[1] * f[1] + momentum[2] * f[2]
    squares = f[0] * f[0] + f[1] * f[1] + f[2] * f[2]
    energy = (moments[4] + moments[7] + moments[9] - 2.0 * dots + density * squares) / 3.0
    fields_out[3] = base[3] + COUPLING * (energy - density * f[3])
    stress = [moments[4 + s] for s in range(6)]
    slope_z = [along_z(stress[s], 1) - along_z(stress[s], -1) for s in (2, 4, 5)]

    faces_wait(*stress_args)
    for s in range(6):
        if s < 5:
            fill(4 + s, stress[s], stress_recv, s)
    fresh = []
    for row in range(3):
        sx, sy, _ = PAIR_INDEX[row]
        slope = along_x(4 + sx, 1) - along_x(4 + sx, -1) + slope_z[row]
        slope = slope + along_y(4 + sy, 1) - along_y(4 + sy, -1)
        value = base[row] - (0.5 * STRESS_GAIN) * slope
        fields_out[row] = value
        fresh.append(split3(value))

    def sampled(hot, c):
        return dot(hot, fresh[c][0]) + dot(hot, fresh[c][1]) + dot(hot, fresh[c][2])

    for c in range(3):
        w = lanes(sampled(pencil_hot, c), where_a)
        third = second_a[c] + RELAXATION * (w - second_a[c])
        for j in range(cap):
            back_send[pl.ds(c * cap + j, n, stride=back_rows), :] = third[j * n : (j + 1) * n]
    all_start(*back_args)
    own = pl.ds(pl.multiple_of(me * back_rows, 8), back_rows)
    back_recv[own, :] = back_send[own, :]
    for c in range(3):
        w = lanes(sampled(home_hot, c), where)
        now = second_ref[c]
        second_ref[c] = live * (now + RELAXATION * (w - now))
    all_wait(*back_args)
    for c in range(3):
        returned = jnp.concatenate(
            [back_recv[pl.ds(c * cap + j, n, stride=back_rows), :] for j in range(cap)], axis=0
        )
        speed_out[c] = jnp.where(moved, live * pick(to_block, returned), second_ref[c])

    all_sent(*pay_args)
    faces_sent(*face_args)
    faces_sent(*stress_args)
    all_sent(*back_args)


def shards(
    flow_speed_field,
    thermal_field,
    walker_speed_vectors,
    walker_statistical_mass,
    gaussian_samples,
    walker_strip_position,
    group_active_tally,
    group_resident_strip,
    migrating_group_table,
    target_processor_slot,
    entered_strip_slot,
):
    n = lax.axis_size("yz")
    n_gx = lax.axis_size("gx")
    X, Y, Z = thermal_field.shape
    blocks, slots = walker_statistical_mass.shape
    moving = migrating_group_table.shape[0]
    cap = 2 * moving // n
    received = n * cap
    rows = -(-SENT * cap // 8) * 8
    back_rows = -(-3 * cap // 8) * 8
    vmem = pl.BlockSpec(memory_space=pltpu.VMEM)
    fields, velocity = pl.pallas_call(
        functools.partial(kernel, n, n_gx, (X, Y, Z)),
        out_shape=(
            jax.ShapeDtypeStruct((4, X * Y, Z), F32),
            jax.ShapeDtypeStruct((3, blocks, slots), F32),
        ),
        in_specs=[vmem] * 11,
        out_specs=(vmem, vmem),
        scratch_shapes=[
            pltpu.VMEM((max(blocks, received) * PITCH, slots), F32),
            pltpu.VMEM((max(blocks, received) * PITCH, Z), F32),
            pltpu.VMEM((3, blocks, slots), F32),
            pltpu.VMEM((received, slots), jnp.int32),
            pltpu.VMEM((MOMENTS, X * Y, Z), F32),
            pltpu.VMEM((9, X + 2, 24, Z), F32),
            pltpu.VMEM((4, 4, 8, Z), F32),
            pltpu.VMEM((4, 4, 8, Z), F32),
            pltpu.VMEM((4, 6, 8, Z), F32),
            pltpu.VMEM((4, 6, 8, Z), F32),
            pltpu.VMEM((n * rows, slots), F32),
            pltpu.VMEM((n * rows, slots), F32),
            pltpu.VMEM((n * back_rows, slots), F32),
            pltpu.VMEM((n * back_rows, slots), F32),
            pltpu.SemaphoreType.DMA((n,)),
            pltpu.SemaphoreType.DMA((n,)),
            pltpu.SemaphoreType.DMA((4,)),
            pltpu.SemaphoreType.DMA((4,)),
            pltpu.SemaphoreType.DMA((4,)),
            pltpu.SemaphoreType.DMA((4,)),
            pltpu.SemaphoreType.DMA((n,)),
            pltpu.SemaphoreType.DMA((n,)),
        ],
        compiler_params=pltpu.CompilerParams(collective_id=0, has_side_effects=True),
    )(
        flow_speed_field.reshape(3, X * Y, Z),
        thermal_field.reshape(X * Y, Z),
        walker_speed_vectors,
        walker_statistical_mass,
        gaussian_samples.reshape(6, blocks, slots),
        walker_strip_position,
        group_active_tally.reshape(1, blocks),
        group_resident_strip.reshape(1, blocks),
        migrating_group_table.reshape(1, moving),
        target_processor_slot.reshape(1, moving),
        entered_strip_slot.reshape(1, moving),
    )
    return fields.reshape(4, X, Y, Z), velocity


def solution(mesh):
    return jax.shard_map(
        shards,
        mesh=mesh,
        in_specs=(
            P(None, "gx", "yz", None),
            P("gx", "yz", None),
            P(None, ("gx", "yz"), None),
            P(("gx", "yz"), None),
            P(None, None, ("gx", "yz"), None),
            P(("gx", "yz"), None),
            P(("gx", "yz")),
            P(("gx", "yz")),
            P(("gx", "yz")),
            P(("gx", "yz"), None),
            P(("gx", "yz")),
        ),
        out_specs=(P(None, "gx", "yz", None), P(None, ("gx", "yz"), None)),
        check_vma=False,
    )
```

time: 103 us -> 26.1 us (0.25)
  matrix products: 32.7 us -> 0 us
  starting transfers between devices: 31.6 us -> 0 us
  Pallas kernels: 0 us -> 23 us
  waiting for transfers between devices: 18.9 us -> 0 us
  local copies, waits for them, and re-layouts: 11.4 us -> 2.29 us
  other arithmetic: 5.86 us -> 0 us
    dot_general x16 -> x0, matrix products: 32.7 us -> none  [the longest x7 20.9 us: at_one_group(): return jnp.einsum('gsz,cgz->cgs', onehot, values, precision=HIGHEST)]
    pallas_call x0 -> x1, Pallas kernels: none -> 23 us  [shards(): pl.pallas_call(functools.partial(kernel, n, n_gx, (X, Y, Z)), out_shape=(...]
    all_to_all x4 -> x0, starting transfers between devices: 21.4 us -> none  [the longest x1 7.28 us: shards(): lax.all_to_all(slot_pencil.reshape(1, yz_count, capacity), 'yz', split_ax...]
    all_to_all x4 -> x0, waiting for transfers between devices: 16.1 us -> none  [the longest x1 6.13 us: shards(): lax.all_to_all(third_velocity[:, block_count:].reshape(3, yz_count, capac...]
    ppermute x4 -> x0, starting transfers between devices: 10.2 us -> none  [the longest x2 7.58 us: with_halo(): lax.ppermute(lax.slice_in_dim(block, block.shape[dim] - width, None, axis...]
    scatter x5 -> x0, local copies, waits for them, and re-layouts: 4.64 us -> none  [the longest x1 1.24 us: shards(): out_cells = jnp.zeros((1, received, slots), jnp.int32).at[0, slot_of].set...]
    ppermute x4 -> x0, waiting for transfers between devices: 2.84 us -> none  [the longest x2 2.57 us: with_halo(): lax.ppermute(lax.slice_in_dim(block, block.shape[dim] - width, None, axis...]
    gather x4 -> x0, local copies, waits for them, and re-layouts: 2.33 us -> none  [the longest x1 0.59 us: shards(): first_velocity[:, migrating_group_table]]
  transfers between devices with their start and end apart: 8 -> 0, of which waited for: 6 -> 0; matrix products, arithmetic and copies ran while one was open for 20% -> 0% of each run, Pallas kernels for 0% -> 0%
where the time goes in v1:
time: 26.1 us; the launch traced here: 25.9 us
  Pallas kernels  23 us (88%)
  local copies, waits for them, and re-layouts  2.29 us (9%)
  between operations  0.65 us (2%)
    pallas_call x1, Pallas kernels, shards(): pl.pallas_call(functools.partial(kernel, n, n_gx, (X, Y, Z)), out_shape=(...  23 us
    unnamed x4, local copies, waits for them, and re-layouts  2.29 us

profile of v1, /device:TPU:0, one launch (start us, length us, event | category | flops | bytes accessed | tf_op | source)
XLA Modules:
  0.0 25.9 jit_solution(12790994620547056192)
XLA Ops:
  0.6 23.0 %shard_map.122 = (f32[4,64,128]{2,1,0:T(8,128)}, f32[3,128,128]{2,1,0:T(8,128)}) custom-call(f32[3,64,128]{2,1,0:T(8,128)} %bitcast.11, f32[64,128]{1,0:T(8,128)} %bitcast.12, f32[3,128,128]{2,1,0:T(8,128)} %speed.1, f32[128,128]{1,0:T(8,128)} %mass.1, f32[6,128,128]{2,1,0:T(8,128)} %bitcast.9, s32[128,128]{1,0:T(8,128)} %cells.1, s32[1,128]{1,0:T(1,128)} %bitcast.13, ...), custom_call_target="tpu_custom_call" | custom-call | tf_op jit(solution)/shard_map/pallas_call | solution.py:419
  23.6 0.0 copy-start
  23.6 1.6 %copy.15 = f32[4,8,8,128]{3,2,1,0:T(8,128)} copy(f32[4,8,8,128]{3,2,1,0:T(8,128)} %bitcast.10) | data formatting | bytes 262144
  25.3 0.0 copy-done
  25.3 0.7 %copy.16 = f32[3,128,128]{2,1,0:T(8,128)} copy(f32[3,128,128]{2,1,0:T(8,128)S(1)} %copy-done) | data formatting | bytes 393216
Async XLA Ops:
  23.6 1.6 %copy-start = (f32[3,128,128]{2,1,0:T(8,128)S(1)}, f32[3,128,128]{2,1,0:T(8,128)}, u32[]{:S(2)}) copy-start(f32[3,128,128]{2,1,0:T(8,128)} %get-tuple-element.9) | copy-start | bytes 589828

commit v2 on v1

--- a/solution.py
+++ b/solution.py
@@ -17,6 +17,7 @@
 MOMENTS = 10
 PITCH = 16
 SENT = 9
+LOAD_ORDER = (6, 7, 8, 9, 10, 0, 1, 5, 2, 3, 4)
 MESH = pl.DeviceIdType.MESH
 BF16 = jnp.bfloat16
 F32 = jnp.float32
@@ -87,19 +88,11 @@
     n,
     n_gx,
     spans,
-    flow,
-    heat,
-    speed,
-    mass,
-    noise,
-    cells,
-    tally,
-    home,
-    table,
-    target,
-    entered,
-    fields_out,
-    speed_out,
+    *refs,
+):
+    sources, (fields_out, speed_out), held, load_s = refs[:11], refs[11:13], refs[13:24], refs[24]
+    flow, heat, speed, mass, noise, cells, tally, home, table, target, entered = held
+    (
     v_ref,
     pb_ref,
     second_ref,
@@ -122,7 +115,11 @@
     stress_r,
     back_s,
     back_r,
-):
+    ) = refs[25:]
+    loads = [
+        pltpu.make_async_copy(source, kept, load_s.at[i])
+        for i, (source, kept) in enumerate(zip(sources, held))
+    ]
     X, Y, Z = spans
     pencils = X * Y
     blocks, slots = mass.shape
@@ -133,7 +130,10 @@
     back_rows = back_send.shape[0] // n
     gx = lax.axis_index("gx")
     me = lax.axis_index("yz")
-    peers = [(i, lax.rem(me + i, n), lax.rem(me + n - i, n)) for i in range(1, n)]
+    order = sorted(range(1, n), key=lambda i: abs(2 * i - n))
+    peers = [(i, lax.rem(me + i, n), lax.rem(me + n - i, n)) for i in order]
+    for i in LOAD_ORDER:
+        loads[i].start()
 
     barrier = pltpu.get_barrier_semaphore()
     for _, peer, _ in peers:
@@ -225,6 +225,9 @@
 
     pay_args = (out_ref, in_ref, rows, out_s, out_r)
     back_args = (back_send, back_recv, back_rows, back_s, back_r)
+
+    for load in loads:
+        load.wait()
 
     for c in range(4):
         grid = flow.at[c] if c < 3 else heat
@@ -415,16 +418,31 @@
     received = n * cap
     rows = -(-SENT * cap // 8) * 8
     back_rows = -(-3 * cap // 8) * 8
+    operands = (
+        flow_speed_field.reshape(3, X * Y, Z),
+        thermal_field.reshape(X * Y, Z),
+        walker_speed_vectors,
+        walker_statistical_mass,
+        gaussian_samples.reshape(6, blocks, slots),
+        walker_strip_position,
+        group_active_tally.reshape(1, blocks),
+        group_resident_strip.reshape(1, blocks),
+        migrating_group_table.reshape(1, moving),
+        target_processor_slot.reshape(1, moving),
+        entered_strip_slot.reshape(1, moving),
+    )
     vmem = pl.BlockSpec(memory_space=pltpu.VMEM)
     fields, velocity = pl.pallas_call(
         functools.partial(kernel, n, n_gx, (X, Y, Z)),
         out_shape=(
-            jax.ShapeDtypeStruct((4, X * Y, Z), F32),
-            jax.ShapeDtypeStruct((3, blocks, slots), F32),
+            pltpu.VMEM((4, X * Y, Z), F32),
+            pltpu.VMEM((3, blocks, slots), F32),
         ),
-        in_specs=[vmem] * 11,
+        in_specs=[pl.BlockSpec(memory_space=pltpu.HBM)] * 11,
         out_specs=(vmem, vmem),
-        scratch_shapes=[
+        scratch_shapes=[pltpu.VMEM(x.shape, x.dtype) for x in operands]
+        + [pltpu.SemaphoreType.DMA((11,))]
+        + [
             pltpu.VMEM((max(blocks, received) * PITCH, slots), F32),
             pltpu.VMEM((max(blocks, received) * PITCH, Z), F32),
             pltpu.VMEM((3, blocks, slots), F32),
@@ -448,20 +466,10 @@
             pltpu.SemaphoreType.DMA((n,)),
             pltpu.SemaphoreType.DMA((n,)),
         ],
-        compiler_params=pltpu.CompilerParams(collective_id=0, has_side_effects=True),
-    )(
-        flow_speed_field.reshape(3, X * Y, Z),
-        thermal_field.reshape(X * Y, Z),
-        walker_speed_vectors,
-        walker_statistical_mass,
-        gaussian_samples.reshape(6, blocks, slots),
-        walker_strip_position,
-        group_active_tally.reshape(1, blocks),
-        group_resident_strip.reshape(1, blocks),
-        migrating_group_table.reshape(1, moving),
-        target_processor_slot.reshape(1, moving),
-        entered_strip_slot.reshape(1, moving),
-    )
+        compiler_params=pltpu.CompilerParams(
+            collective_id=0, has_side_effects=True, vmem_limit_bytes=32 * 1024 * 1024
+        ),
+    )(*(pltpu.with_memory_space_constraint(x, pltpu.HBM) for x in operands))
     return fields.reshape(4, X, Y, Z), velocity
 
 

time: 26.1 us -> 23.3 us (0.89)
  Pallas kernels: 23 us -> 21.1 us
  local copies, waits for them, and re-layouts: 2.29 us -> 1.33 us
    pallas_call x1, Pallas kernels: 23 us -> 21.1 us  [shards(): pl.pallas_call(functools.partial(kernel, n, n_gx, (X, Y, Z)), out_shape=(...]
    unnamed x4 -> x2, local copies, waits for them, and re-layouts: 2.29 us -> 1.33 us
where the time goes in v2:
time: 23.3 us; the launch traced here: 23.1 us
  Pallas kernels  21.1 us (91%)
  local copies, waits for them, and re-layouts  1.33 us (6%)
  between operations  0.64 us (3%)
    pallas_call x1, Pallas kernels, shards(): pl.pallas_call(functools.partial(kernel, n, n_gx, (X, Y, Z)), out_shape=(...  21.1 us
    unnamed x2, local copies, waits for them, and re-layouts  1.33 us

profile of v2, /device:TPU:0, one launch (start us, length us, event | category | flops | bytes accessed | tf_op | source)
XLA Modules:
  0.0 23.1 jit_solution(5807697894550090886)
XLA Ops:
  0.6 21.1 %shard_map.122 = (f32[4,64,128]{2,1,0:T(8,128)S(1)}, f32[3,128,128]{2,1,0:T(8,128)S(1)}) custom-call(f32[3,64,128]{2,1,0:T(8,128)} %bitcast.11, f32[64,128]{1,0:T(8,128)} %bitcast.12, f32[3,128,128]{2,1,0:T(8,128)} %refs_2_.1, f32[128,128]{1,0:T(8,128)} %refs_3_.1, f32[6,128,128]{2,1,0:T(8,128)} %bitcast.10, s32[128,128]{1,0:T(8,128)} %refs_5_.1, ...), custom_call_target="tpu_custom_call" | custom-call | tf_op jit(solution)/shard_map/pallas_call | solution.py:435
  21.8 0.7 %copy.15 = f32[4,8,8,128]{3,2,1,0:T(8,128)} copy(f32[4,8,8,128]{3,2,1,0:T(8,128)S(1)} %bitcast.9) | data formatting | bytes 262144
  22.4 0.7 %copy.16 = f32[3,128,128]{2,1,0:T(8,128)} copy(f32[3,128,128]{2,1,0:T(8,128)S(1)} %get-tuple-element.7) | data formatting | bytes 393216

commit v3 on v2

--- a/solution.py
+++ b/solution.py
@@ -1,4 +1,5 @@
 import functools
+import math
 
 import jax
 import jax.numpy as jnp
@@ -17,6 +18,7 @@
 MOMENTS = 10
 PITCH = 16
 SENT = 9
+UNROLL = 32
 LOAD_ORDER = (6, 7, 8, 9, 10, 0, 1, 5, 2, 3, 4)
 MESH = pl.DeviceIdType.MESH
 BF16 = jnp.bfloat16
@@ -194,37 +196,37 @@
     face_args = (face_send, face_recv, face_s, face_r)
     stress_args = (stress_send, stress_recv, stress_s, stress_r)
 
-    def all_copy(i, peer, send, recv, height, send_sem, recv_sem):
+    def all_copy(i, peer, send, recv, height, pitch, send_sem, recv_sem):
         return pltpu.make_async_remote_copy(
-            src_ref=send.at[pl.ds(pl.multiple_of(peer * height, 8), height), :],
-            dst_ref=recv.at[pl.ds(pl.multiple_of(me * height, 8), height), :],
+            src_ref=send.at[pl.ds(pl.multiple_of(peer * pitch, 8), height), :],
+            dst_ref=recv.at[pl.ds(pl.multiple_of(me * pitch, 8), height), :],
             send_sem=send_sem.at[i],
             recv_sem=recv_sem.at[i],
             device_id={"yz": peer},
             device_id_type=MESH,
         )
 
-    def all_start(send, recv, height, send_sem, recv_sem):
+    def all_start(send, recv, height, pitch, send_sem, recv_sem):
         for i, peer, _ in peers:
-            all_copy(i, peer, send, recv, height, send_sem, recv_sem).start()
-
-    def all_wait(send, recv, height, send_sem, recv_sem):
+            all_copy(i, peer, send, recv, height, pitch, send_sem, recv_sem).start()
+
+    def all_wait(send, recv, height, pitch, send_sem, recv_sem):
         for i, _, source in peers:
             pltpu.make_async_remote_copy(
-                src_ref=send.at[pl.ds(pl.multiple_of(source * height, 8), height), :],
-                dst_ref=recv.at[pl.ds(pl.multiple_of(source * height, 8), height), :],
+                src_ref=send.at[pl.ds(pl.multiple_of(source * pitch, 8), height), :],
+                dst_ref=recv.at[pl.ds(pl.multiple_of(source * pitch, 8), height), :],
                 send_sem=send_sem.at[i],
                 recv_sem=recv_sem.at[i],
                 device_id={"yz": source},
                 device_id_type=MESH,
             ).wait_recv()
 
-    def all_sent(send, recv, height, send_sem, recv_sem):
+    def all_sent(send, recv, height, pitch, send_sem, recv_sem):
         for i, peer, _ in peers:
-            all_copy(i, peer, send, recv, height, send_sem, recv_sem).wait_send()
-
-    pay_args = (out_ref, in_ref, rows, out_s, out_r)
-    back_args = (back_send, back_recv, back_rows, back_s, back_r)
+            all_copy(i, peer, send, recv, height, pitch, send_sem, recv_sem).wait_send()
+
+    pay_args = (out_ref, in_ref, SENT * cap, rows, out_s, out_r)
+    back_args = (back_send, back_recv, 3 * cap, back_rows, back_s, back_r)
 
     for load in loads:
         load.wait()
@@ -282,7 +284,7 @@
     for c in range(3):
         second_ref[c] = second[c]
     put_terms(v_ref, blocks, jnp.where(moved, 0.0, weight), second)
-    deposit(blocks, 8, v_ref, cells, pb_ref)
+    deposit(blocks, math.gcd(blocks, UNROLL), v_ref, cells, pb_ref)
     for k in range(MOMENTS):
         moments[k] = pick(home_t, pb_ref[pl.ds(k, blocks, stride=PITCH), :])
 
@@ -303,7 +305,7 @@
     spread_a = jnp.sqrt((1.0 - DECAY * DECAY) * temp_a)
     second_a = [drift(got[c], u_a[c], spread_a, got[4 + c]) for c in range(3)]
     put_terms(v_ref, received, got[3], second_a)
-    deposit(received, 8, v_ref, cells_a, pb_ref)
+    deposit(received, math.gcd(received, UNROLL), v_ref, cells_a, pb_ref)
     for k in range(MOMENTS - 1, -1, -1):
         total = moments[k] + pick(pencil_t, pb_ref[pl.ds(k, received, stride=PITCH), :])
         moments[k] = total
@@ -394,6 +396,17 @@
     faces_sent(*face_args)
     faces_sent(*stress_args)
     all_sent(*back_args)
+
+
+def put_out(fields, velocity, fields_out, velocity_out, sems):
+    copies = (
+        pltpu.make_async_copy(fields, fields_out, sems.at[0]),
+        pltpu.make_async_copy(velocity, velocity_out, sems.at[1]),
+    )
+    for copy in copies:
+        copy.start()
+    for copy in copies:
+        copy.wait()
 
 
 def shards(
@@ -470,6 +483,18 @@
             collective_id=0, has_side_effects=True, vmem_limit_bytes=32 * 1024 * 1024
         ),
     )(*(pltpu.with_memory_space_constraint(x, pltpu.HBM) for x in operands))
+    hbm = pl.BlockSpec(memory_space=pltpu.HBM)
+    fields, velocity = pl.pallas_call(
+        put_out,
+        out_shape=(
+            jax.ShapeDtypeStruct((4, X * Y, Z), F32),
+            jax.ShapeDtypeStruct((3, blocks, slots), F32),
+        ),
+        in_specs=[vmem, vmem],
+        out_specs=(hbm, hbm),
+        scratch_shapes=[pltpu.SemaphoreType.DMA((2,))],
+        compiler_params=pltpu.CompilerParams(vmem_limit_bytes=32 * 1024 * 1024),
+    )(fields, velocity)
     return fields.reshape(4, X, Y, Z), velocity
 
 

time: 23.3 us -> 21.7 us (0.931)
  local copies, waits for them, and re-layouts: 1.33 us -> 0 us
    unnamed x2 -> x0, local copies, waits for them, and re-layouts: 1.33 us -> none
    pallas_call x1, Pallas kernels: 21.1 us -> 20.2 us  [shards(): pl.pallas_call(functools.partial(kernel, n, n_gx, (X, Y, Z)), out_shape=(...]
    pallas_call x0 -> x1, Pallas kernels: none -> 0.74 us  [shards(): pl.pallas_call(put_out, out_shape=(jax.ShapeDtypeStruct((4, X * Y, Z), F3...]
where the time goes in v3:
time: 21.7 us; the launch traced here: 21.6 us
  Pallas kernels  20.9 us (96%)
  between operations  0.64 us (3%)
    pallas_call x1, Pallas kernels, shards(): pl.pallas_call(functools.partial(kernel, n, n_gx, (X, Y, Z)), out_shape=(...  20.2 us
    pallas_call x1, Pallas kernels, shards(): pl.pallas_call(put_out, out_shape=(jax.ShapeDtypeStruct((4, X * Y, Z), F3...  0.74 us

profile of v3, /device:TPU:0, one launch (start us, length us, event | category | flops | bytes accessed | tf_op | source)
XLA Modules:
  0.0 21.6 jit_solution(9408012251899976251)
XLA Ops:
  0.6 20.2 %shard_map.122 = (f32[4,64,128]{2,1,0:T(8,128)S(1)}, f32[3,128,128]{2,1,0:T(8,128)S(1)}) custom-call(f32[3,64,128]{2,1,0:T(8,128)} %bitcast.10, f32[64,128]{1,0:T(8,128)} %bitcast.11, f32[3,128,128]{2,1,0:T(8,128)} %refs_2_.1, f32[128,128]{1,0:T(8,128)} %refs_3_.1, f32[6,128,128]{2,1,0:T(8,128)} %bitcast.9, s32[128,128]{1,0:T(8,128)} %refs_5_.1, ...), custom_call_target="tpu_custom_call" | custom-call | tf_op jit(solution)/shard_map/pallas_call | solution.py:448
  20.9 0.7 %shard_map.123 = (f32[4,64,128]{2,1,0:T(8,128)}, f32[3,128,128]{2,1,0:T(8,128)}) custom-call(f32[4,64,128]{2,1,0:T(8,128)S(1)} %get-tuple-element.6.fields, f32[3,128,128]{2,1,0:T(8,128)S(1)} %get-tuple-element.7.velocity), custom_call_target="tpu_custom_call" | custom-call | tf_op jit(solution)/shard_map/pallas_call | solution.py:487
